TPU v7x, 128 devices: a whole 4x4x4 slice. The times are simulated.
128 devices in a mesh: dp: 16 (over z_lo, x, core), group: 8 (over z_hi, y).
Axes of the slice: x: 4, y: 4, z: 4 (z_hi: 2, z_lo: 2; z = z_hi * 2 + z_lo), core: 2. Of those that a mesh axis runs over, the one named last changes fastest.
Arguments:
- activations: bfloat16 [2048, 8192], P('dp'), may hold values from -6 to 6
- out_grads: bfloat16 [2048, 28672], P('dp', 'group'), may hold values from -6 to 6
- basis_in: bfloat16 [16, 512, 512], P('dp'), may hold values from -0.25 to 0.25
- basis_out: bfloat16 [56, 512, 512], P('group'), may hold values from -0.25 to 0.25
- query_grads: bfloat16 [28672, 3, 8192], P('group', None, 'dp'), may hold values from -6 to 6
- eigenvalues: bfloat16 [28672, 8192], P('group', 'dp'), may hold values from 0.049804688 to 5
- doc_ids: int32 [2048], replicated, may hold values from 0 to 63, never falling along the last dimension, each value on 1 to 64 neighbouring positions
Outputs:
- doc_scores: float32 [3, 64], replicated
Inputs may be any that keep to these rules, and one draw needn't show every extreme that they name: doc_ids never falls along the tokens; every document 0 to 63 has 1 to 64 tokens, and one has exactly 64.
All inputs are finite; a program needn't handle non-finite values.
Results may differ from a plain program's by a relative error of at most 0.0055.
Values may be sent and summed in bfloat16 or wider, within the bound.
No kernel may reach another device: no remote copies, remote signals or barrier semaphores. Data moves between devices by JAX's collectives and lax.ppermute only.
A program may use at most 192 MiB of HBM per device.

v0:
```python
import math
import jax
import jax.numpy as jnp
from jax import lax
from jax.sharding import PartitionSpec as P

D = 8192
FF = 28672
DOC_AVG = 32
damping = 0.1


def rotate_rows(rows_in, basis):
    row_count = rows_in.shape[0]
    nblocks = basis.shape[0]
    block_width = basis.shape[1]
    shaped = rows_in.reshape(row_count, nblocks, block_width)
    turned = jnp.einsum("tnb,nbc->tnc", shaped, basis, preferred_element_type=jnp.float32)
    return turned.reshape(row_count, nblocks * block_width).astype(jnp.bfloat16)


def on_device(activations, out_grads, basis_in, basis_out, query_grads, eigenvalues, doc_ids):
    blocks_in = lax.all_to_all(activations, "dp", split_axis=1, concat_axis=0, tiled=True)
    rotated_in = rotate_rows(blocks_in, basis_in)
    out_cols = query_grads.shape[0]
    queries = query_grads.shape[1]
    in_cols = query_grads.shape[2]
    scaled = (
        query_grads.astype(jnp.float32) / (eigenvalues.astype(jnp.float32)[:, None, :] + damping)
    ).astype(jnp.bfloat16)
    scaled = scaled.reshape(out_cols, queries * in_cols)
    doc_total = doc_ids.shape[0] // DOC_AVG
    doc_range = jnp.arange(doc_total, dtype=jnp.int32)
    rotated_out = rotate_rows(out_grads, basis_out)
    grad_piece = lax.all_gather(rotated_out, "dp", axis=0, tiled=True)
    piece_rows = grad_piece.shape[0]
    projected = jnp.dot(grad_piece, scaled, preferred_element_type=jnp.float32).reshape(
        piece_rows, queries, in_cols
    )
    token_scores = jnp.sum(projected * rotated_in.astype(jnp.float32)[:, None, :], axis=2)
    membership = (doc_ids[:, None] == doc_range[None, :]).astype(jnp.float32)
    local_scores = jnp.dot(
        token_scores.T,
        membership,
        precision=lax.Precision.HIGHEST,
        preferred_element_type=jnp.float32,
    )
    doc_scores = lax.psum(local_scores, ("dp", "group"))
    return doc_scores * (1.0 / math.sqrt(FF * D))


def solution(mesh):
    return jax.shard_map(
        on_device,
        mesh=mesh,
        in_specs=(
            P("dp", None),
            P("dp", "group"),
            P("dp", None, None),
            P("group", None, None),
            P("group", None, "dp"),
            P("group", "dp"),
            P(),
        ),
        out_specs=P(),
        check_vma=False,
    )
```

profile of v0, /device:TPU:1, one launch (start us, length us, event | category | flops | bytes accessed | tf_op | source)
XLA Modules:
  0.0 226.4 jit_solution(9948356858457873738)
XLA Ops:
  6.5 0.0 copy-start
  6.5 0.0 all-gather.2.cloned.1.call-start
  6.5 1.6 copy.25
  8.2 3.3 %convolution_convert_fusion.1 = bf16[7,512,128]{2,1,0:T(8,128)(2,1)S(1)} fusion(bf16[7,512,512]{2,1,0:T(8,128)(2,1)} %param.10, bf16[128,7,512]{0,2,1:T(8,128)(2,1)S(1)} %bitcast.40), kind=kOutput, calls=%fused_computation.10 | convolution fusion | flops 470220800 | bytes 5505024 | tf_op jit(solution)/shard_map/tnb,nbc->tnc/dot_general | solution.py:18
  11.5 1.3 copy.28
  12.8 0.0 all-gather.2.cloned.1.call-update
  12.8 4.1 %copy.31 = bf16[128,8192]{0,1:T(8,128)(2,1)} copy(bf16[128,8192]{1,0:T(8,128)(2,1)} %param.7) | data formatting | bytes 4194304 | tf_op args[0]
  16.9 7.2 %all-to-all-start = ((bf16[128,16,512]{0,2,1:T(8,128)(2,1)}), bf16[128,16,512]{0,2,1:T(8,128)(2,1)S(1)}, u32[]{:S(2)}, u32[]{:S(2)}) async-start(bf16[128,16,512]{0,2,1:T(8,128)(2,1)} %bitcast.38), calls=%async_computation | async-start | bytes 4194304 | tf_op jit(solution)/shard_map/all_to_all | solution.py:23
  24.1 6.4 %convert_add_fusion = f32[3584,512]{1,0:T(8,128)} fusion(bf16[3584,512]{1,0:T(8,128)(2,1)} %param.12), kind=kLoop, calls=%fused_computation.6 | loop fusion | flops 3670016 | bytes 11010048 | tf_op jit(solution)/shard_map/add | solution.py:29
  30.5 8.4 %copy.30 = f32[3584,512]{0,1:T(8,128)} copy(f32[3584,512]{1,0:T(8,128)} %convert_add_fusion) | data formatting | bytes 14680064 | tf_op jit(solution)/shard_map/add | solution.py:29
  38.9 14.7 %copy.29 = bf16[3584,3,512]{0,2,1:T(8,128)(2,1)} copy(bf16[3584,3,512]{2,0,1:T(8,128)(2,1)} %param.11) | data formatting | bytes 22020096 | tf_op args[4]
  53.6 18.2 %all-to-all-done = bf16[128,16,512]{0,2,1:T(8,128)(2,1)S(1)} async-done(((bf16[128,16,512]{0,2,1:T(8,128)(2,1)}), bf16[128,16,512]{0,2,1:T(8,128)(2,1)S(1)}, u32[]{:S(2)}, u32[]{:S(2)}) %all-to-all-start) | async-done | bytes 2097184 | tf_op jit(solution)/shard_map/all_to_all | solution.py:23
  71.8 2.6 %copy.32 = bf16[16,128,512]{2,1,0:T(8,128)(2,1)} copy(bf16[16,128,512]{1,2,0:T(8,128)(2,1)S(1)} %bitcast.37) | data formatting | bytes 4194304 | tf_op jit(solution)/shard_map/all_to_all | solution.py:23
  74.4 0.0 copy-done
  74.4 4.9 %convert_bitcast_fusion = f32[2048,512]{0,1:T(8,128)} fusion(bf16[2048,512]{1,0:T(8,128)(2,1)} %bitcast.41, bf16[1,512,512]{2,1,0:T(8,128)(2,1)S(1)} %copy-done), kind=kOutput, calls=%fused_computation.7 | convolution fusion | flops 1075838976 | bytes 6815744 | tf_op jit(solution)/shard_map/tnb,nbc->tnc/dot_general | solution.py:18
  79.4 0.0 copy-start.2
  79.4 40.7 %all-gather.2.cloned.1.call-done = bf16[2048,3584]{1,0:T(8,128)(2,1)} async-done(((bf16[128,3584]{1,0:T(8,128)(2,1)}), bf16[2048,3584]{1,0:T(8,128)(2,1)}) %all-gather.2.cloned.1.call-update) | async-done | bytes 14680080 | tf_op jit(solution)/shard_map/all_gather | solution.py:35
  120.1 0.0 copy-start.1
  120.1 31.9 %multiply_reduce_fusion = f32[2048,3]{0,1:T(4,128)S(1)} fusion(f32[2048,512]{0,1:T(8,128)} %convert_bitcast_fusion, bf16[3584,3,512]{0,2,1:T(8,128)(2,1)} %copy.29, f32[3584,512]{0,1:T(8,128)} %copy.30, bf16[2048,3584]{1,0:T(8,128)(2,1)} %all-gather.2.cloned.1.call-done), kind=kOutput, calls=%fused_computation.3 | convolution fusion | flops 22571378688 | bytes 37249024 | tf_op jit(solution)/shard_map/dot_general | solution.py:37
  152.0 0.0 copy-done.2
  152.0 0.6 fusion.10
  152.6 66.3 %psum.7 = f32[3,64]{1,0:T(4,128)S(1)} all-reduce(f32[3,64]{1,0:T(4,128)S(1)} %fusion.10), channel_id=1, replica_groups=mesh['dp'=16,'group'=8] {'dp','group'}, use_global_device_ids=true, to_apply=%region_1.0 | all-reduce | flops 192 | bytes 1536 | tf_op jit(solution)/shard_map/psum | solution.py:48
  218.9 0.6 broadcast_multiply_fusion
  219.5 0.0 copy-done.1
Async XLA Ops:
  6.5 67.9 %copy-start = (bf16[1,512,512]{2,1,0:T(8,128)(2,1)S(1)}, bf16[1,512,512]{2,1,0:T(8,128)(2,1)}, u32[]{:S(2)}) copy-start(bf16[1,512,512]{2,1,0:T(8,128)(2,1)} %param.9) | copy-start | bytes 1572868
  6.5 113.6 %all-gather.2.cloned.1.call-start = ((), (), s32[]{:S(2)}) async-start(), calls=%async_computation.1 | async-start | bytes 15597568 | tf_op jit(solution)/shard_map/all_gather | solution.py:35
  16.9 54.9 %all-to-all-start = ((bf16[128,16,512]{0,2,1:T(8,128)(2,1)}), bf16[128,16,512]{0,2,1:T(8,128)(2,1)S(1)}, u32[]{:S(2)}, u32[]{:S(2)}) async-start(bf16[128,16,512]{0,2,1:T(8,128)(2,1)} %bitcast.38), calls=%async_computation | async-start | bytes 4194304 | tf_op jit(solution)/shard_map/all_to_all | solution.py:23
  79.4 72.7 %copy-start.2 = (s32[2048]{0:T(1024)S(1)}, s32[2048]{0:T(1024)}, u32[]{:S(2)}) copy-start(s32[2048]{0:T(1024)} %param.13) | copy-start | bytes 24580
  120.1 99.4 %copy-start.1 = (bf16[1,512,512]{2,1,0:T(8,128)(2,1)S(1)}, bf16[1,512,512]{2,1,0:T(8,128)(2,1)}, u32[]{:S(2)}) copy-start(bf16[1,512,512]{2,1,0:T(8,128)(2,1)} %param.9) | copy-start | bytes 1572868
Sparse Core Ops, SparseCore 0:
  12.9 107.1 all-gather.1
where the time goes:
time: 227 us; the launch traced here: 226 us
  blocking collectives  66.3 us (29%)
  waiting for transfers between devices  58.9 us (26%)
  matrix products  40.7 us (18%)
  local copies, waits for them, and re-layouts  32.8 us (14%)
  between operations  13.4 us (6%)
  starting transfers between devices  7.16 us (3%)
  other arithmetic  6.97 us (3%)
    psum x1, blocking collectives, on_device(): doc_scores = lax.psum(local_scores, ('dp', 'group'))  66.3 us
    all_gather x1, waiting for transfers between devices, on_device(): grad_piece = lax.all_gather(rotated_out, 'dp', axis=0, tiled=True)  40.7 us
    dot_general x1, matrix products, on_device(): jnp.dot(grad_piece, scaled, preferred_element_type=jnp.float32)  31.9 us
    unnamed x9, local copies, waits for them, and re-layouts  20.4 us
    all_to_all x1, waiting for transfers between devices, on_device(): lax.all_to_all(activations, 'dp', split_axis=1, concat_axis=0, tiled=True)  18.2 us
    add x1, local copies, waits for them, and re-layouts, on_device(): eigenvalues.astype(jnp.float32)[:, None, :] + damping  8.43 us
    dot_general x2, matrix products, rotate_rows(): jnp.einsum('tnb,nbc->tnc', shaped, basis, preferred_element_type=jnp.floa...  8.25 us
    all_to_all x1, starting transfers between devices, on_device(): lax.all_to_all(activations, 'dp', split_axis=1, concat_axis=0, tiled=True)  7.16 us
  transfers between devices with their start and end apart: 2, of which 2 were waited for; matrix products, arithmetic and copies ran while one was open for 18% of the time, Pallas kernels for 0%

commit v1 on v0

--- a/solution.py
+++ b/solution.py
@@ -8,6 +8,11 @@
 FF = 28672
 DOC_AVG = 32
 damping = 0.1
+
+
+def by_each_axis(value, axis_one, axis_two):
+    inner = lax.psum(value, axis_one)
+    return lax.psum(inner, axis_two)
 
 
 def rotate_rows(rows_in, basis):
@@ -45,7 +50,7 @@
         precision=lax.Precision.HIGHEST,
         preferred_element_type=jnp.float32,
     )
-    doc_scores = lax.psum(local_scores, ("dp", "group"))
+    doc_scores = by_each_axis(local_scores, "group", "dp")
     return doc_scores * (1.0 / math.sqrt(FF * D))
 
 

time: 227 us -> 213 us (0.938)
  blocking collectives: 66.3 us -> 51.7 us
    psum x1 -> x2, blocking collectives: 66.3 us -> 51.7 us  [the longest x1 30.5 us: by_each_axis(): return lax.psum(inner, axis_two)]
  transfers between devices with their start and end apart: 2 -> 2, of which waited for: 2 -> 2; matrix products, arithmetic and copies ran while one was open for 18% -> 20% of each run, Pallas kernels for 0% -> 0%
where the time goes in v1:
time: 213 us; the launch traced here: 212 us
  waiting for transfers between devices  58.8 us (28%)
  blocking collectives  51.7 us (24%)
  matrix products  40.7 us (19%)
  local copies, waits for them, and re-layouts  33 us (15%)
  between operations  13.4 us (6%)
  starting transfers between devices  7.16 us (3%)
  other arithmetic  6.98 us (3%)
    all_gather x1, waiting for transfers between devices, on_device(): grad_piece = lax.all_gather(rotated_out, 'dp', axis=0, tiled=True)  40.8 us
    dot_general x1, matrix products, on_device(): jnp.dot(grad_piece, scaled, preferred_element_type=jnp.float32)  31.9 us
    psum x1, blocking collectives, by_each_axis(): return lax.psum(inner, axis_two)  30.5 us
    psum x1, blocking collectives, by_each_axis(): inner = lax.psum(value, axis_one)  21.1 us
    unnamed x9, local copies, waits for them, and re-layouts  20.7 us
    all_to_all x1, waiting for transfers between devices, on_device(): lax.all_to_all(activations, 'dp', split_axis=1, concat_axis=0, tiled=True)  18 us
    add x1, local copies, waits for them, and re-layouts, on_device(): eigenvalues.astype(jnp.float32)[:, None, :] + damping  8.38 us
    dot_general x2, matrix products, rotate_rows(): jnp.einsum('tnb,nbc->tnc', shaped, basis, preferred_element_type=jnp.floa...  8.25 us
  transfers between devices with their start and end apart: 2, of which 2 were waited for; matrix products, arithmetic and copies ran while one was open for 20% of the time, Pallas kernels for 0%

profile of v1, /device:TPU:1, one launch (start us, length us, event | category | flops | bytes accessed | tf_op | source)
XLA Modules:
  0.0 211.8 jit_solution(17007521605197737938)
XLA Ops:
  6.5 0.0 copy-start
  6.5 0.0 all-gather.2.cloned.1.call-start
  6.5 1.6 copy.25
  8.2 3.3 %convolution_convert_fusion.1 = bf16[7,512,128]{2,1,0:T(8,128)(2,1)S(1)} fusion(bf16[7,512,512]{2,1,0:T(8,128)(2,1)} %param.10, bf16[128,7,512]{0,2,1:T(8,128)(2,1)S(1)} %bitcast.40), kind=kOutput, calls=%fused_computation.10 | convolution fusion | flops 470220800 | bytes 5505024 | tf_op jit(solution)/shard_map/tnb,nbc->tnc/dot_general | solution.py:23
  11.5 1.3 copy.28
  12.8 0.0 all-gather.2.cloned.1.call-update
  12.9 4.1 %copy.31 = bf16[128,8192]{0,1:T(8,128)(2,1)} copy(bf16[128,8192]{1,0:T(8,128)(2,1)} %param.7) | data formatting | bytes 4194304 | tf_op args[0]
  16.9 7.2 %all-to-all-start = ((bf16[128,16,512]{0,2,1:T(8,128)(2,1)}), bf16[128,16,512]{0,2,1:T(8,128)(2,1)S(1)}, u32[]{:S(2)}, u32[]{:S(2)}) async-start(bf16[128,16,512]{0,2,1:T(8,128)(2,1)} %bitcast.38), calls=%async_computation | async-start | bytes 4194304 | tf_op jit(solution)/shard_map/all_to_all | solution.py:28
  24.1 6.4 %convert_add_fusion = f32[3584,512]{1,0:T(8,128)} fusion(bf16[3584,512]{1,0:T(8,128)(2,1)} %param.12), kind=kLoop, calls=%fused_computation.6 | loop fusion | flops 3670016 | bytes 11010048 | tf_op jit(solution)/shard_map/add | solution.py:34
  30.5 8.4 %copy.30 = f32[3584,512]{0,1:T(8,128)} copy(f32[3584,512]{1,0:T(8,128)} %convert_add_fusion) | data formatting | bytes 14680064 | tf_op jit(solution)/shard_map/add | solution.py:34
  38.9 15.0 %copy.29 = bf16[3584,3,512]{0,2,1:T(8,128)(2,1)} copy(bf16[3584,3,512]{2,0,1:T(8,128)(2,1)} %param.11) | data formatting | bytes 22020096 | tf_op args[4]
  53.9 18.0 %all-to-all-done = bf16[128,16,512]{0,2,1:T(8,128)(2,1)S(1)} async-done(((bf16[128,16,512]{0,2,1:T(8,128)(2,1)}), bf16[128,16,512]{0,2,1:T(8,128)(2,1)S(1)}, u32[]{:S(2)}, u32[]{:S(2)}) %all-to-all-start) | async-done | bytes 2097184 | tf_op jit(solution)/shard_map/all_to_all | solution.py:28
  71.9 2.6 %copy.32 = bf16[16,128,512]{2,1,0:T(8,128)(2,1)} copy(bf16[16,128,512]{1,2,0:T(8,128)(2,1)S(1)} %bitcast.37) | data formatting | bytes 4194304 | tf_op jit(solution)/shard_map/all_to_all | solution.py:28
  74.5 0.0 copy-done
  74.5 4.9 %convert_bitcast_fusion = f32[2048,512]{0,1:T(8,128)} fusion(bf16[2048,512]{1,0:T(8,128)(2,1)} %bitcast.41, bf16[1,512,512]{2,1,0:T(8,128)(2,1)S(1)} %copy-done), kind=kOutput, calls=%fused_computation.7 | convolution fusion | flops 1075838976 | bytes 6815744 | tf_op jit(solution)/shard_map/tnb,nbc->tnc/dot_general | solution.py:23
  79.4 0.0 copy-start.2
  79.4 40.8 %all-gather.2.cloned.1.call-done = bf16[2048,3584]{1,0:T(8,128)(2,1)} async-done(((bf16[128,3584]{1,0:T(8,128)(2,1)}), bf16[2048,3584]{1,0:T(8,128)(2,1)}) %all-gather.2.cloned.1.call-update) | async-done | bytes 14680080 | tf_op jit(solution)/shard_map/all_gather | solution.py:40
  120.1 31.9 %multiply_reduce_fusion = f32[2048,3]{0,1:T(4,128)S(1)} fusion(f32[2048,512]{0,1:T(8,128)} %convert_bitcast_fusion, bf16[3584,3,512]{0,2,1:T(8,128)(2,1)} %copy.29, f32[3584,512]{0,1:T(8,128)} %copy.30, bf16[2048,3584]{1,0:T(8,128)(2,1)} %all-gather.2.cloned.1.call-done), kind=kOutput, calls=%fused_computation.3 | convolution fusion | flops 22571378688 | bytes 37249024 | tf_op jit(solution)/shard_map/dot_general | solution.py:42
  152.1 0.0 copy-done.2
  152.1 0.6 fusion.10
  152.7 21.1 %psum.14 = f32[3,64]{1,0:T(4,128)S(1)} all-reduce(f32[3,64]{1,0:T(4,128)S(1)} %fusion.10), channel_id=1, replica_groups=mesh['dp'=16,'group'=8] {'group'}, use_global_device_ids=true, to_apply=%region_1.0 | all-reduce | flops 192 | bytes 1536 | tf_op jit(solution)/shard_map/psum | solution.py:14
  173.8 30.5 %psum.15 = f32[3,64]{1,0:T(4,128)S(1)} all-reduce(f32[3,64]{1,0:T(4,128)S(1)} %psum.14), channel_id=1, replica_groups=mesh['dp'=16,'group'=8] {'dp'}, use_global_device_ids=true, to_apply=%region_2.0 | all-reduce | flops 192 | bytes 1536 | tf_op jit(solution)/shard_map/psum | solution.py:15
  204.3 0.6 broadcast_multiply_fusion
  204.9 0.0 copy-done.1
  (1 shorter events, 0.0 us)
Async XLA Ops:
  6.5 67.9 %copy-start = (bf16[1,512,512]{2,1,0:T(8,128)(2,1)S(1)}, bf16[1,512,512]{2,1,0:T(8,128)(2,1)}, u32[]{:S(2)}) copy-start(bf16[1,512,512]{2,1,0:T(8,128)(2,1)} %param.9) | copy-start | bytes 1572868
  6.5 113.6 %all-gather.2.cloned.1.call-start = ((), (), s32[]{:S(2)}) async-start(), calls=%async_computation.1 | async-start | bytes 15597568 | tf_op jit(solution)/shard_map/all_gather | solution.py:40
  16.9 54.9 %all-to-all-start = ((bf16[128,16,512]{0,2,1:T(8,128)(2,1)}), bf16[128,16,512]{0,2,1:T(8,128)(2,1)S(1)}, u32[]{:S(2)}, u32[]{:S(2)}) async-start(bf16[128,16,512]{0,2,1:T(8,128)(2,1)} %bitcast.38), calls=%async_computation | async-start | bytes 4194304 | tf_op jit(solution)/shard_map/all_to_all | solution.py:28
  79.4 72.7 %copy-start.2 = (s32[2048]{0:T(1024)S(1)}, s32[2048]{0:T(1024)}, u32[]{:S(2)}) copy-start(s32[2048]{0:T(1024)} %param.13) | copy-start | bytes 24580
  120.1 84.8 %copy-start.1 = (bf16[1,512,512]{2,1,0:T(8,128)(2,1)S(1)}, bf16[1,512,512]{2,1,0:T(8,128)(2,1)}, u32[]{:S(2)}) copy-start(bf16[1,512,512]{2,1,0:T(8,128)(2,1)} %param.9) | copy-start | bytes 1572868
Sparse Core Ops, SparseCore 0:
  13.0 107.1 all-gather.1

commit v2 on v0

--- a/solution.py
+++ b/solution.py
@@ -1,3 +1,4 @@
+import functools
 import math
 import jax
 import jax.numpy as jnp
@@ -8,6 +9,17 @@
 FF = 28672
 DOC_AVG = 32
 damping = 0.1
+
+
+def resolve_vectors_all(local_array, ax_name):
+    before = lax.axis_size(ax_name)
+    field_out = jnp.stack([local_array] * before)
+    all_rows = lax.all_to_all(field_out, ax_name, 0, 0)
+    r2 = jnp.concatenate(all_rows, 0)
+    return r2
+
+
+yards_check = functools.partial(resolve_vectors_all, ax_name="dp")
 
 
 def rotate_rows(rows_in, basis):
@@ -32,7 +44,7 @@
     doc_total = doc_ids.shape[0] // DOC_AVG
     doc_range = jnp.arange(doc_total, dtype=jnp.int32)
     rotated_out = rotate_rows(out_grads, basis_out)
-    grad_piece = lax.all_gather(rotated_out, "dp", axis=0, tiled=True)
+    grad_piece = yards_check(rotated_out)
     piece_rows = grad_piece.shape[0]
     projected = jnp.dot(grad_piece, scaled, preferred_element_type=jnp.float32).reshape(
         piece_rows, queries, in_cols

time: 227 us -> 350 us (1.54)
  waiting for transfers between devices: 58.9 us -> 180 us
  between operations: 13.4 us -> 0.04 us
  local copies, waits for them, and re-layouts: 32.8 us -> 40.6 us
  starting transfers between devices: 7.16 us -> 12.5 us
    all_to_all x0 -> x1, waiting for transfers between devices: none -> 159 us  [resolve_vectors_all(): all_rows = lax.all_to_all(field_out, ax_name, 0, 0)]
    all_gather x1 -> x0, waiting for transfers between devices: 40.7 us -> none  [on_device(): grad_piece = lax.all_gather(rotated_out, 'dp', axis=0, tiled=True)]
    another operation x0 -> x1, local copies, waits for them, and re-layouts: none -> 7.79 us  [resolve_vectors_all(): field_out = jnp.stack([local_array] * before)]
    all_to_all x0 -> x1, starting transfers between devices: none -> 5.35 us  [resolve_vectors_all(): all_rows = lax.all_to_all(field_out, ax_name, 0, 0)]
    unnamed x9 -> x11, local copies, waits for them, and re-layouts: 20.4 us -> 20.5 us
  transfers between devices with their start and end apart: 2 -> 2, of which waited for: 2 -> 2; matrix products, arithmetic and copies ran while one was open for 18% -> 12% of each run, Pallas kernels for 0% -> 0%
where the time goes in v2:
time: 350 us; the launch traced here: 349 us
  waiting for transfers between devices  180 us (51%)
  blocking collectives  67.6 us (19%)
  matrix products  40.9 us (12%)
  local copies, waits for them, and re-layouts  40.6 us (12%)
  starting transfers between devices  12.5 us (4%)
  other arithmetic  6.7 us (2%)
    all_to_all x1, waiting for transfers between devices, resolve_vectors_all(): all_rows = lax.all_to_all(field_out, ax_name, 0, 0)  159 us
    psum x1, blocking collectives, on_device(): doc_scores = lax.psum(local_scores, ('dp', 'group'))  67.6 us
    dot_general x1, matrix products, on_device(): jnp.dot(grad_piece, scaled, preferred_element_type=jnp.float32)  31.9 us
    all_to_all x1, waiting for transfers between devices, on_device(): lax.all_to_all(activations, 'dp', split_axis=1, concat_axis=0, tiled=True)  21.4 us
    unnamed x11, local copies, waits for them, and re-layouts  20.5 us
    add x1, local copies, waits for them, and re-layouts, on_device(): eigenvalues.astype(jnp.float32)[:, None, :] + damping  8.45 us
    dot_general x2, matrix products, rotate_rows(): jnp.einsum('tnb,nbc->tnc', shaped, basis, preferred_element_type=jnp.floa...  8.41 us
    another operation x1, local copies, waits for them, and re-layouts, resolve_vectors_all(): field_out = jnp.stack([local_array] * before)  7.79 us
  transfers between devices with their start and end apart: 2, of which 2 were waited for; matrix products, arithmetic and copies ran while one was open for 12% of the time, Pallas kernels for 0%

profile of v2, /device:TPU:1, one launch (start us, length us, event | category | flops | bytes accessed | tf_op | source)
XLA Modules:
  0.0 348.8 jit_solution(2012826776918193946)
XLA Ops:
  0.0 0.0 copy-start
  0.0 4.2 %copy.33 = bf16[128,8192]{0,1:T(8,128)(2,1)} copy(bf16[128,8192]{1,0:T(8,128)(2,1)} %param.7) | data formatting | bytes 4194304 | tf_op args[0]
  4.2 7.2 %all-to-all-start.1 = ((bf16[128,16,512]{0,2,1:T(8,128)(2,1)}), bf16[128,16,512]{0,2,1:T(8,128)(2,1)S(1)}, u32[]{:S(2)}, u32[]{:S(2)}) async-start(bf16[128,16,512]{0,2,1:T(8,128)(2,1)} %bitcast.37), calls=%async_computation.1 | async-start | bytes 4194304 | tf_op jit(solution)/shard_map/all_to_all | solution.py:35
  11.4 0.0 copy-done.2
  11.4 1.3 copy.27
  12.7 3.6 %convolution_convert_fusion.1 = bf16[7,512,128]{2,1,0:T(8,128)(2,1)S(1)} fusion(bf16[7,512,512]{2,1,0:T(8,128)(2,1)} %param.10, bf16[128,7,512]{0,2,1:T(8,128)(2,1)} %bitcast.39), kind=kOutput, calls=%fused_computation.9 | convolution fusion | flops 470220800 | bytes 5505024 | tf_op jit(solution)/shard_map/tnb,nbc->tnc/dot_general | solution.py:30
  16.2 1.3 copy.30
  17.5 21.4 %all-to-all-done.1 = bf16[128,16,512]{0,2,1:T(8,128)(2,1)S(1)} async-done(((bf16[128,16,512]{0,2,1:T(8,128)(2,1)}), bf16[128,16,512]{0,2,1:T(8,128)(2,1)S(1)}, u32[]{:S(2)}, u32[]{:S(2)}) %all-to-all-start.1) | async-done | bytes 2097184 | tf_op jit(solution)/shard_map/all_to_all | solution.py:35
  39.0 7.8 %stack.2 = bf16[16,128,3584]{2,1,0:T(8,128)(2,1)} broadcast(bf16[128,3584]{1,0:T(8,128)(2,1)} %copy.30), dimensions={1,2} | broadcast | bytes 15597568 | tf_op jit(solution)/shard_map/stack | solution.py:16
  46.8 5.4 %all-to-all-start = ((bf16[16,128,3584]{2,1,0:T(8,128)(2,1)}), bf16[16,128,3584]{2,1,0:T(8,128)(2,1)}, u32[]{:S(2)}, u32[]{:S(2)}) async-start(bf16[16,128,3584]{2,1,0:T(8,128)(2,1)} %stack.2), calls=%async_computation | async-start | bytes 29360128 | tf_op jit(solution)/shard_map/all_to_all | solution.py:17
  52.1 6.1 %convert_add_fusion = f32[3584,512]{1,0:T(8,128)} fusion(bf16[3584,512]{1,0:T(8,128)(2,1)} %param.12), kind=kLoop, calls=%fused_computation.5 | loop fusion | flops 3670016 | bytes 11010048 | tf_op jit(solution)/shard_map/add | solution.py:41
  58.2 8.4 %copy.32 = f32[3584,512]{0,1:T(8,128)} copy(f32[3584,512]{1,0:T(8,128)} %convert_add_fusion) | data formatting | bytes 14680064 | tf_op jit(solution)/shard_map/add | solution.py:41
  66.7 15.0 %copy.31 = bf16[3584,3,512]{0,2,1:T(8,128)(2,1)} copy(bf16[3584,3,512]{2,0,1:T(8,128)(2,1)} %param.11) | data formatting | bytes 22020096 | tf_op args[4]
  81.7 2.6 copy.34
  84.2 0.0 copy-done
  84.2 4.8 %convert_bitcast_fusion = f32[2048,512]{0,1:T(8,128)} fusion(bf16[2048,512]{1,0:T(8,128)(2,1)} %bitcast.40, bf16[1,512,512]{2,1,0:T(8,128)(2,1)S(1)} %copy-done), kind=kOutput, calls=%fused_computation.6 | convolution fusion | flops 1075838976 | bytes 6815744 | tf_op jit(solution)/shard_map/tnb,nbc->tnc/dot_general | solution.py:30
  89.1 159.1 %all-to-all-done = bf16[16,128,3584]{2,1,0:T(8,128)(2,1)} async-done(((bf16[16,128,3584]{2,1,0:T(8,128)(2,1)}), bf16[16,128,3584]{2,1,0:T(8,128)(2,1)}, u32[]{:S(2)}, u32[]{:S(2)}) %all-to-all-start) | async-done | bytes 14680096 | tf_op jit(solution)/shard_map/all_to_all | solution.py:17
  248.1 0.0 copy-start.3
  248.1 31.9 %multiply_reduce_fusion = f32[2048,3]{0,1:T(4,128)S(1)} fusion(f32[2048,512]{0,1:T(8,128)} %convert_bitcast_fusion, bf16[2048,3584,1]{1,0,2:T(8,128)(2,1)} %bitcast.4, bf16[3584,3,512]{0,2,1:T(8,128)(2,1)} %copy.31, f32[3584,512]{0,1:T(8,128)} %copy.32), kind=kOutput, calls=%fused_computation.1 | convolution fusion | flops 22571378688 | bytes 37249024 | tf_op jit(solution)/shard_map/dot_general | solution.py:49
  280.1 0.0 copy-done.3
  280.1 0.6 fusion.7
  280.7 67.6 %psum.7 = f32[3,64]{1,0:T(4,128)S(1)} all-reduce(f32[3,64]{1,0:T(4,128)S(1)} %fusion.7), channel_id=1, replica_groups=mesh['dp'=16,'group'=8] {'dp','group'}, use_global_device_ids=true, to_apply=%region_1.0 | all-reduce | flops 192 | bytes 1536 | tf_op jit(solution)/shard_map/psum | solution.py:60
  348.3 0.6 broadcast_multiply_fusion
  348.8 0.0 copy-done.1
  (2 shorter events, 0.0 us)
Async XLA Ops:
  0.0 84.2 %copy-start = (bf16[1,512,512]{2,1,0:T(8,128)(2,1)S(1)}, bf16[1,512,512]{2,1,0:T(8,128)(2,1)}, u32[]{:S(2)}) copy-start(bf16[1,512,512]{2,1,0:T(8,128)(2,1)} %param.9) | copy-start | bytes 1572868
  0.0 11.4 %copy-start.2 = (bf16[128,3584]{1,0:T(8,128)(2,1)S(1)}, bf16[128,3584]{1,0:T(8,128)(2,1)}, u32[]{:S(2)}) copy-start(bf16[128,3584]{1,0:T(8,128)(2,1)} %param.8) | copy-start | bytes 2752516
  4.2 34.8 %all-to-all-start.1 = ((bf16[128,16,512]{0,2,1:T(8,128)(2,1)}), bf16[128,16,512]{0,2,1:T(8,128)(2,1)S(1)}, u32[]{:S(2)}, u32[]{:S(2)}) async-start(bf16[128,16,512]{0,2,1:T(8,128)(2,1)} %bitcast.37), calls=%async_computation.1 | async-start | bytes 4194304 | tf_op jit(solution)/shard_map/all_to_all | solution.py:35
  46.8 201.4 %all-to-all-start = ((bf16[16,128,3584]{2,1,0:T(8,128)(2,1)}), bf16[16,128,3584]{2,1,0:T(8,128)(2,1)}, u32[]{:S(2)}, u32[]{:S(2)}) async-start(bf16[16,128,3584]{2,1,0:T(8,128)(2,1)} %stack.2), calls=%async_computation | async-start | bytes 29360128 | tf_op jit(solution)/shard_map/all_to_all | solution.py:17
  248.1 31.9 %copy-start.3 = (s32[2048]{0:T(1024)S(1)}, s32[2048]{0:T(1024)}, u32[]{:S(2)}) copy-start(s32[2048]{0:T(1024)} %param.13) | copy-start | bytes 24580
  248.1 100.7 %copy-start.1 = (bf16[1,512,512]{2,1,0:T(8,128)(2,1)S(1)}, bf16[1,512,512]{2,1,0:T(8,128)(2,1)}, u32[]{:S(2)}) copy-start(bf16[1,512,512]{2,1,0:T(8,128)(2,1)} %param.9) | copy-start | bytes 1572868
